TPU v7x, 128 devices: a whole 4x4x4 slice. The times are simulated.
128 devices in a mesh: sx: 8 (over z, core), sy: 8 (over x_lo, y), rep: 2 (over x_hi).
Axes of the slice: x: 4 (x_hi: 2, x_lo: 2; x = x_hi * 2 + x_lo), y: 4, z: 4, core: 2. Of those that a mesh axis runs over, the one named last changes fastest.
Arguments:
- volume: bfloat16 [2, 32, 16, 128, 256], P('rep', None, 'sx', 'sy'), may hold values from -6 to 6
- first_kernel: bfloat16 [64, 32, 3, 3, 3], replicated, may hold values from -0.21875 to 0.21875
- first_bias: float32 [64], replicated, may hold values from -3 to 3
- second_kernel: bfloat16 [128, 64, 3, 3, 3], P('sy'), may hold values from -0.15625 to 0.15625
- second_bias: float32 [128], P('sy'), may hold values from -3 to 3
- cotangent: bfloat16 [2, 128, 8, 64, 128], P('rep', 'sy', 'sx'), may hold values from -6 to 6
Outputs:
- second_out: float32 [2, 128, 8, 64, 128], P('rep', 'sy', 'sx')
- grad_first_kernel: float32 [64, 32, 3, 3, 3], replicated
- grad_first_bias: float32 [64], replicated
- grad_second_kernel: float32 [128, 64, 3, 3, 3], P('sy')
- grad_second_bias: float32 [128], P('sy')
All inputs are finite; a program needn't handle non-finite values.
Results may differ from a plain program's by a relative error of at most 0.0045.
Values may be sent and summed in bfloat16 or wider, within the bound.
A program may use at most 128 MiB of HBM per device.

v0:
```python
import math
import jax
import jax.numpy as jnp
from jax import lax
from jax.sharding import PartitionSpec as P


def padded_2(cells, sides, width):
    for axis, dim in sides:
        count = lax.axis_size(axis)
        ends = count - 1
        head = lax.slice_in_dim(cells, 0, width, axis=dim)
        tail = lax.slice_in_dim(cells, cells.shape[dim] - width, cells.shape[dim], axis=dim)
        cells = jnp.concatenate(
            [
                lax.ppermute(tail, axis, [(i, (i + 1) % count) for i in range(ends)]),
                cells,
                lax.ppermute(head, axis, [((i + 1) % count, i) for i in range(ends)]),
            ],
            axis=dim,
        )
    return cells


def convolve(padded, kernel, z_pad):
    return lax.conv_general_dilated(
        padded[None],
        kernel,
        (1, 1, 1),
        ((0, 0), (0, 0), (z_pad, z_pad)),
        dimension_numbers=("NCDHW", "OIDHW", "NCDHW"),
        preferred_element_type=jnp.float32,
    )[0]


def weight_terms(cotan, padded):
    cells_x, cells_y, cells_z = (cotan.shape[1], cotan.shape[2], cotan.shape[3])
    terms = []
    for i in range(3):
        for j in range(3):
            for k in range(3):
                piece = padded[:, i : i + cells_x, j : j + cells_y, k : k + cells_z]
                terms.append(
                    jnp.einsum("oxyz,cxyz->oc", cotan, piece, preferred_element_type=jnp.float32)
                )
    stacked = jnp.stack(terms).reshape(3, 3, 3, cotan.shape[0], padded.shape[0])
    return stacked.transpose(3, 4, 0, 1, 2)


def pool_mean(field):
    chans, cells_x, cells_y, cells_z = field.shape
    blocks = field.astype(jnp.float32).reshape(
        chans, cells_x // 2, 2, cells_y // 2, 2, cells_z // 2, 2
    )
    return jnp.mean(blocks, axis=(2, 4, 6))


def per_device(volume, first_kernel, first_bias, second_kernel, second_bias, cotangent):
    source = volume[0]
    cotan = cotangent[0]
    half_x, half_y, half_z = (source.shape[1] // 2, source.shape[2] // 2, source.shape[3] // 2)
    count = (
        lax.axis_size("rep") * lax.axis_size("sx") * lax.axis_size("sy") * half_x * half_y * half_z
    )
    scale = 1.0 / math.sqrt(count)
    rimmed = padded_2(source, (("sx", 1), ("sy", 2)), 1)
    input_pad = jnp.pad(rimmed, ((0, 0), (0, 0), (0, 0), (1, 1)))
    pre = convolve(input_pad, first_kernel, 0) + first_bias[:, None, None, None]
    act = jnp.where(pre > 0, pre, 0.3 * pre)
    pooled = pool_mean(act).astype(jnp.bfloat16)
    pooled_x = padded_2(pooled, (("sx", 1),), 1)
    gathered = lax.all_gather(pooled_x, "sy", axis=2, tiled=True)
    pooled_pad = jnp.pad(gathered, ((0, 0), (0, 0), (1, 1), (1, 1)))
    second = convolve(pooled_pad, second_kernel, 0) + second_bias[:, None, None, None]
    second_out = second.astype(jnp.float32)
    local_w2 = weight_terms(cotan, pooled_pad)
    local_b2 = jnp.sum(cotan.astype(jnp.float32), axis=(1, 2, 3))
    cot_x = padded_2(cotan, (("sx", 1),), 1)
    cot_pad = jnp.pad(cot_x, ((0, 0), (0, 0), (1, 1), (1, 1)))
    flipped = second_kernel.transpose(1, 0, 2, 3, 4)[:, :, ::-1, ::-1, ::-1]
    partial_back = convolve(cot_pad, flipped, 0)
    back = lax.psum_scatter(partial_back, "sy", scatter_dimension=2, tiled=True)
    summed_w2, summed_b2 = lax.psum((local_w2, local_b2), ("sx", "rep"))
    spread = jnp.repeat(jnp.repeat(jnp.repeat(back, 2, axis=1), 2, axis=2), 2, axis=3)
    grad_pre = (spread * 0.125 * jnp.where(pre > 0, 1.0, 0.3)).astype(jnp.bfloat16)
    local_w1 = weight_terms(grad_pre, input_pad)
    local_b1 = jnp.sum(grad_pre.astype(jnp.float32), axis=(1, 2, 3))
    summed_w1, summed_b1 = lax.psum((local_w1, local_b1), ("sx", "sy", "rep"))
    return (
        second_out[None],
        scale * summed_w1,
        scale * summed_b1,
        scale * summed_w2,
        scale * summed_b2,
    )


def solution(mesh):
    placed = (
        P("rep", None, "sx", "sy", None),
        P(),
        P(),
        P("sy", None, None, None, None),
        P("sy"),
        P("rep", "sy", "sx", None, None),
    )
    return jax.shard_map(
        per_device,
        mesh=mesh,
        in_specs=placed,
        out_specs=(
            P("rep", "sy", "sx", None, None),
            P(),
            P(),
            P("sy", None, None, None, None),
            P("sy"),
        ),
        check_vma=False,
    )
```

profile of v0, /device:TPU:1, one launch (start us, length us, event | category | flops | bytes accessed | tf_op | source)
XLA Modules:
  0.0 535.4 jit_solution(5171773666828313169)
XLA Ops:
  8.7 4.9 collective-permute-start.6
  15.5 4.2 collective-permute-done.6
  19.7 4.4 collective-permute-done.7
  25.9 6.1 %copy.331 = bf16[16,3,66,1,8,17]{0,4,5,2,1,3:T(8,128)(2,1)} copy(bf16[16,3,66,1,8,17]{2,0,5,4,1,3:T(8,128)(2,1)S(1)} %bitcast.640) | data formatting | bytes 1723392 | tf_op jit(solution)/shard_map/conv_general_dilated | solution.py:26
  33.4 9.5 %broadcast_select_fusion = f32[1,64,8,17,64]{4,2,3,1,0:T(8,128)S(1)} fusion(pred[8,17]{0,1:T(8,128)(4,1)S(1)} %copy-done.20, bf16[16,64,3,3,3]{1,0,4,3,2:T(8,128)(2,1)S(1)} %copy-done.17, bf16[16,3,66,1,7,2]{0,4,5,2,1,3:T(8,128)(2,1)S(1)} %slice.266, bf16[16,3,66,1,8,17]{0,4,5,2,1,3:T(8,128)(2,1)} %copy.331), kind=kOutput, calls=%fused_computation.70 | convolution fusion | flops 484742656 | bytes 3234056 | tf_op jit(solution)/shard_map/conv_general_dilated | solution.py:26
  43.7 2.6 slice_bitcast_fusion.1
  49.6 2.4 collective-permute-start.1
  52.9 4.7 collective-permute-done.1
  57.6 3.2 collective-permute-start.2
  63.5 4.2 collective-permute-done.3
  69.6 5.4 %reshape.246 = bf16[32,4,18,1,8,33]{5,4,0,2,1,3:T(8,128)(2,1)} reshape(bf16[32,4,18,1,264]{4,0,2,1,3:T(8,128)(2,1)S(1)} %pad.15) | data formatting | bytes 2433024 | tf_op jit(solution)/shard_map/conv_general_dilated | solution.py:26
  75.0 9.3 %copy.321 = bf16[32,4,18,1,8,33]{0,4,5,2,1,3:T(8,128)(2,1)} copy(bf16[32,4,18,1,8,33]{5,4,0,2,1,3:T(8,128)(2,1)} %reshape.246) | data formatting | bytes 2433024 | tf_op jit(solution)/shard_map/conv_general_dilated | solution.py:26
  85.4 12.4 %compare_select_fusion = (f32[2,16,8,33,64]{4,2,3,1,0:T(8,128)}, f32[2,16,8,33,64]{4,2,3,1,0:T(8,128)S(1)}, f32[2,16,8,33,64]{4,2,3,1,0:T(8,128)}) fusion(f32[64]{0:T(128)S(1)} %copy-done.15, bf16[64,32,3,3,3]{0,1,4,3,2:T(8,128)(2,1)S(1)} %copy-done, bf16[32,4,18,1,7,2]{0,4,5,2,1,3:T(8,128)(2,1)S(1)} %slice.262, bf16[32,4,18,1,8,33]{0,4,5,2,1,3:T(8,128)(2,1)} %copy.321, ...), kind=kOutput, calls=%fused_computation.44 | convolution fusion | flops 941395968 | bytes 7880200 | tf_op jit(solution)/shard_map/conv_general_dilated | solution.py:26
  99.0 3.3 reduce_sum.36
  104.2 3.3 collective-permute-start.4
  109.5 3.1 copy.334
  114.9 5.1 copy.419
  120.0 5.1 copy.349
  126.7 11.1 %select_maximum_fusion = bf16[32,4,18,258]{3,0,2,1:T(8,128)(2,1)} fusion(bf16[32,4,1,256]{3,0,2,1:T(8,128)(2,1)S(1)} %collective-permute-done.3, bf16[32,4,1,256]{3,0,2,1:T(8,128)(2,1)S(1)} %collective-permute-done.2, bf16[32,1,16,256]{3,0,2,1:T(8,128)(2,1)S(1)} %collective-permute-done.1, bf16[32,2,16,256]{3,0,2,1:T(8,128)(2,1)S(1)} %bitcast.630, ...), kind=kLoop, calls=%fused_computation.77 | loop fusion | flops 10699776 | bytes 2368512 | tf_op jit(solution)/shard_map/concatenate | solution.py:14
  139.5 2.4 copy.333
  141.9 2.4 multiply_convert_fusion
  182.9 36.2 %psum.31 = f32[16]{0:T(128)S(1)} all-reduce(f32[16]{0:T(128)S(1)} %convert_reduce_fusion.1), channel_id=1, replica_groups=mesh['sx'=8,'sy'=8,'rep'=2] {'sx','rep'}, use_global_device_ids=true, to_apply=%region_8.9 | all-reduce | flops 16 | bytes 128 | tf_op jit(solution)/shard_map/psum | solution.py:83
  219.7 66.4 %psum.29 = f32[64]{0:T(128)S(1)} all-reduce(f32[64]{0:T(128)S(1)} %get-tuple-element.30), channel_id=1, replica_groups=mesh['sx'=8,'sy'=8,'rep'=2] {'sx','sy','rep'}, use_global_device_ids=true, to_apply=%region_5.6 | all-reduce | flops 64 | bytes 512 | tf_op jit(solution)/shard_map/psum | solution.py:88
  286.6 41.3 %all-reduce.6.cloned.1.call-done = f32[64,32,3,3,3]{0,1,4,3,2:T(8,128)} async-done(((f32[64,32,3,3,3]{0,1,4,3,2:T(8,128)}), f32[64,32,3,3,3]{0,1,4,3,2:T(8,128)}) %all-reduce.6.cloned.1.call-update) | async-done | bytes 221200 | tf_op jit(solution)/shard_map/psum | solution.py:88
  329.7 40.3 %all-gather.2.cloned.1.call-done = bf16[64,3,64,128]{3,0,2,1:T(8,128)(2,1)} async-done(((bf16[64,3,8,128]{3,0,2,1:T(8,128)(2,1)}), bf16[64,3,64,128]{3,0,2,1:T(8,128)(2,1)}) %all-gather.2.cloned.1.call-update) | async-done | bytes 3145744 | tf_op jit(solution)/shard_map/all_gather | solution.py:72
  385.5 5.5 %pad_bitcast_fusion = bf16[64,3,66,1,130]{4,0,2,1,3:T(8,128)(2,1)} fusion(bf16[64,3,64,128]{3,0,2,1:T(8,128)(2,1)S(1)} %copy-done.2), kind=kLoop, calls=%fused_computation.24 | loop fusion | bytes 6440448 | tf_op jit(solution)/shard_map/broadcast_in_dim | solution.py:27
  391.0 14.8 %copy.420 = bf16[64,3,66,1,130]{2,0,4,1,3:T(8,128)(2,1)} copy(bf16[64,3,66,1,130]{4,0,2,1,3:T(8,128)(2,1)} %pad_bitcast_fusion) | data formatting | bytes 6589440
  405.8 7.5 %pad.17.clone = bf16[64,3,66,1,136]{2,0,4,1,3:T(8,128)(2,1)} pad(bf16[64,3,66,1,130]{2,0,4,1,3:T(8,128)(2,1)} %copy.420, bf16[]{:T(256)} %constant.6.clone.1), padding=0_0x0_0x0_0x0_0x0_6 | pad | bytes 6741506 | tf_op jit(solution)/shard_map/broadcast_in_dim | solution.py:27
  413.3 11.8 %copy.326 = bf16[64,3,66,1,8,17]{0,4,5,2,1,3:T(8,128)(2,1)} copy(bf16[64,3,66,1,8,17]{2,0,5,4,1,3:T(8,128)(2,1)} %bitcast.623) | data formatting | bytes 6893568 | tf_op jit(solution)/shard_map/conv_general_dilated | solution.py:26
  426.5 19.6 %fusion.9 = f32[1,64,8,17,16]{4,2,3,1,0:T(8,128)} fusion(bf16[16,64,3,3,3]{1,0,4,3,2:T(8,128)(2,1)S(1)} %copy-done.18, bf16[64,3,66,1,7,2]{0,4,5,2,1,3:T(8,128)(2,1)S(1)} %slice.264, bf16[64,3,66,1,8,17]{0,4,5,2,1,3:T(8,128)(2,1)} %copy.326), kind=kOutput, calls=%fused_computation.36 | convolution fusion | flops 492853248 | bytes 4413952 | tf_op jit(solution)/shard_map/conv_general_dilated | solution.py:26
  446.1 3.2 copy.327
  450.9 75.9 %all-reduce.8.cloned.1.call-done = f32[16,64,3,3,3]{1,0,4,3,2:T(8,128)} async-done(((f32[16,64,3,3,3]{1,0,4,3,2:T(8,128)}), f32[16,64,3,3,3]{1,0,4,3,2:T(8,128)}) %all-reduce.8.cloned.1.call-update) | async-done | bytes 110608 | tf_op jit(solution)/shard_map/psum | solution.py:83
  (149 shorter events, 89.1 us)
Async XLA Ops:
  7.2 78.2 %copy-start = (bf16[64,32,3,3,3]{0,1,4,3,2:T(8,128)(2,1)S(1)}, bf16[64,32,3,3,3]{0,1,4,3,2:T(8,128)(2,1)}, u32[]{:S(2)}) copy-start(bf16[64,32,3,3,3]{0,1,4,3,2:T(8,128)(2,1)} %param.7) | copy-start | bytes 331780
  7.2 130.7 %reduce-scatter.2.cloned.1.call-start = ((), (), s32[]{:S(2)}) async-start(), calls=%async_computation.2 | async-start | bytes 4718592 | tf_op jit(solution)/shard_map/reduce_scatter | solution.py:82
  8.7 11.0 %collective-permute-start.6 = (bf16[16,1,64,128]{2,0,3,1:T(8,128)(2,1)S(1)}, bf16[16,1,64,128]{2,0,3,1:T(8,128)(2,1)S(1)}, u32[]{:S(2)}, u32[]{:S(2)}) collective-permute-start(bf16[16,1,64,128]{2,0,3,1:T(8,128)(2,1)S(1)} %bitcast.641), channel_id=1, source_target_pairs={{0,16},{16,32},{32,48},{48,64},{64,80},{80,96},{96,112},{1,17},{17... | collective-permute-start | bytes 786440 | tf_op jit(solution)/shard_map/ppermute | solution.py:16
  13.6 10.5 %collective-permute-start.7 = (bf16[16,1,64,128]{2,0,3,1:T(8,128)(2,1)S(1)}, bf16[16,1,64,128]{2,0,3,1:T(8,128)(2,1)S(1)}, u32[]{:S(2)}, u32[]{:S(2)}) collective-permute-start(bf16[16,1,64,128]{2,0,3,1:T(8,128)(2,1)S(1)} %bitcast.642), channel_id=1, source_target_pairs={{16,0},{32,16},{48,32},{64,48},{80,64},{96,80},{112,96},{17,1},{33... | collective-permute-start | bytes 786440 | tf_op jit(solution)/shard_map/ppermute | solution.py:18
  25.9 7.5 %copy-start.17 = (bf16[16,64,3,3,3]{1,0,4,3,2:T(8,128)(2,1)S(1)}, bf16[16,64,3,3,3]{1,0,4,3,2:T(8,128)(2,1)}, u32[]{:S(2)}) copy-start(bf16[16,64,3,3,3]{1,0,4,3,2:T(8,128)(2,1)} %param.9) | copy-start | bytes 165892
  25.9 7.5 %copy-start.20 = (pred[8,17]{0,1:T(8,128)(4,1)S(1)}, pred[8,17]{0,1:T(8,128)(4,1)}, u32[]{:S(2)}) copy-start(pred[8,17]{0,1:T(8,128)(4,1)} %constant.43) | copy-start | bytes 412
  46.3 281.6 %all-reduce.6.cloned.1.call-start = ((), (), s32[]{:S(2)}) async-start(), calls=%async_computation.3 | async-start | bytes 884736 | tf_op jit(solution)/shard_map/psum | solution.py:88
  47.7 5.2 collective-permute-start
  49.6 8.0 %collective-permute-start.1 = (bf16[32,1,16,256]{3,0,2,1:T(8,128)(2,1)S(1)}, bf16[32,1,16,256]{3,0,2,1:T(8,128)(2,1)S(1)}, u32[]{:S(2)}, u32[]{:S(2)}) collective-permute-start(bf16[32,1,16,256]{3,0,2,1:T(8,128)(2,1)S(1)} %get-tuple-element.39), channel_id=1, source_target_pairs={{16,0},{32,16},{48,32},{64,48},{80,64},{96,80},{112,96},{17,1},{33... | collective-permute-start | bytes 786440 | tf_op jit(solution)/shard_map/ppermute | solution.py:18
  52.9 14.9 %copy-start.4 = (bf16[32,1,16,256]{3,0,2,1:T(8,128)(2,1)}, bf16[32,1,16,256]{3,0,2,1:T(8,128)(2,1)S(1)}, u32[]{:S(2)}) copy-start(bf16[32,1,16,256]{3,0,2,1:T(8,128)(2,1)S(1)} %collective-permute-done) | copy-start | bytes 786436
  57.6 5.9 %collective-permute-start.2 = (bf16[32,4,1,256]{3,0,2,1:T(8,128)(2,1)S(1)}, bf16[32,4,1,256]{3,0,2,1:T(8,128)(2,1)S(1)}, u32[]{:S(2)}, u32[]{:S(2)}) collective-permute-start(bf16[32,4,1,256]{3,0,2,1:T(8,128)(2,1)S(1)} %get-tuple-element.36), channel_id=1, source_target_pairs={{0,2},{2,4},{4,6},{6,8},{8,10},{10,12},{12,14},{1,3},{3,5},{5,7},{... | collective-permute-start | bytes 196616 | tf_op jit(solution)/shard_map/ppermute | solution.py:16
  60.8 6.9 %collective-permute-start.3 = (bf16[32,4,1,256]{3,0,2,1:T(8,128)(2,1)S(1)}, bf16[32,4,1,256]{3,0,2,1:T(8,128)(2,1)S(1)}, u32[]{:S(2)}, u32[]{:S(2)}) collective-permute-start(bf16[32,4,1,256]{3,0,2,1:T(8,128)(2,1)S(1)} %get-tuple-element.37), channel_id=1, source_target_pairs={{2,0},{4,2},{6,4},{8,6},{10,8},{12,10},{14,12},{3,1},{5,3},{7,5},{... | collective-permute-start | bytes 196616 | tf_op jit(solution)/shard_map/ppermute | solution.py:18
  75.0 10.4 %copy-start.15 = (f32[64]{0:T(128)S(1)}, f32[64]{0:T(128)}, u32[]{:S(2)}) copy-start(f32[64]{0:T(128)} %param.8) | copy-start | bytes 772
  75.0 10.4 %copy-start.19 = (pred[8,33]{0,1:T(8,128)(4,1)S(1)}, pred[8,33]{0,1:T(8,128)(4,1)}, u32[]{:S(2)}) copy-start(pred[8,33]{0,1:T(8,128)(4,1)} %constant.41) | copy-start | bytes 796
  104.2 76.5 %collective-permute-start.4 = (bf16[64,1,8,128]{3,0,2,1:T(8,128)(2,1)}, bf16[64,1,8,128]{3,0,2,1:T(8,128)(2,1)}, u32[]{:S(2)}, u32[]{:S(2)}) collective-permute-start(bf16[64,1,8,128]{3,0,2,1:T(8,128)(2,1)} %fusion.182), channel_id=1, source_target_pairs={{0,16},{16,32},{32,48},{48,64},{64,80},{80,96},{96,112},{1,17},{17... | collective-permute-start | bytes 393224 | tf_op jit(solution)/shard_map/ppermute | solution.py:16
  107.5 73.2 %collective-permute-start.5 = (bf16[64,1,8,128]{3,0,2,1:T(8,128)(2,1)}, bf16[64,1,8,128]{3,0,2,1:T(8,128)(2,1)}, u32[]{:S(2)}, u32[]{:S(2)}) collective-permute-start(bf16[64,1,8,128]{3,0,2,1:T(8,128)(2,1)} %fusion.182), channel_id=1, source_target_pairs={{16,0},{32,16},{48,32},{64,48},{80,64},{96,80},{112,96},{17,1},{33... | collective-permute-start | bytes 393224 | tf_op jit(solution)/shard_map/ppermute | solution.py:18
  120.0 5.1 copy-start.5
  141.8 2.4 copy-start.7
  141.9 3.7 copy-start.9
  145.5 3.8 copy-start.6
  149.3 3.8 copy-start.8
  151.9 9.2 %slice-start = ((s8[4325376]{0:T(1024)(128)(4,1)}), s8[4194304]{0:T(1024)(128)(4,1)S(1)}, s32[]{:S(2)}) async-start(s8[4325376]{0:T(1024)(128)(4,1)} %bitcast.635), calls=%async_computation.5 | async-start | bytes 8388608
  156.1 5.1 slice-start.1
  161.2 1.1 copy-start.11
  177.3 192.7 %copy-start.3 = (bf16[1,16,1,64,128]{4,3,2,1,0:T(8,128)(2,1)S(1)}, bf16[1,16,1,64,128]{4,3,2,1,0:T(8,128)(2,1)}, u32[]{:S(2)}) copy-start(bf16[1,16,1,64,128]{4,3,2,1,0:T(8,128)(2,1)} %param.11) | copy-start | bytes 786436
  180.7 189.4 %all-gather.2.cloned.1.call-start = ((), (), s32[]{:S(2)}) async-start(), calls=%async_computation.1 | async-start | bytes 3538944 | tf_op jit(solution)/shard_map/all_gather | solution.py:72
  182.6 344.2 %all-reduce.8.cloned.1.call-start = ((), (), s32[]{:S(2)}) async-start(), calls=%async_computation.4 | async-start | bytes 442368 | tf_op jit(solution)/shard_map/psum | solution.py:83
  370.0 2.2 copy-start.2
  413.3 13.2 %copy-start.18 = (bf16[16,64,3,3,3]{1,0,4,3,2:T(8,128)(2,1)S(1)}, bf16[16,64,3,3,3]{1,0,4,3,2:T(8,128)(2,1)}, u32[]{:S(2)}) copy-start(bf16[16,64,3,3,3]{1,0,4,3,2:T(8,128)(2,1)} %param.9) | copy-start | bytes 165892
  446.1 3.2 copy-start.14
  446.1 3.2 copy-start.16
  446.1 82.3 %copy-start.1 = (bf16[64,32,3,3,3]{0,1,4,3,2:T(8,128)(2,1)S(1)}, bf16[64,32,3,3,3]{0,1,4,3,2:T(8,128)(2,1)}, u32[]{:S(2)}) copy-start(bf16[64,32,3,3,3]{0,1,4,3,2:T(8,128)(2,1)} %param.7) | copy-start | bytes 331780
  (3 other events, 2.6 us)
Sparse Core Ops, SparseCore 0:
  46.4 54.4 reduce-scatter.1
  180.8 147.0 all-reduce.5
  330.1 39.8 all-gather.1
  385.7 141.0 all-reduce.7
where the time goes:
time: 545 us; the launch traced here: 535 us
  waiting for transfers between devices  177 us (32%)
  blocking collectives  103 us (19%)
  local copies, waits for them, and re-layouts  97.9 us (18%)
  matrix products  90 us (17%)
  other arithmetic  31.6 us (6%)
  starting transfers between devices  21.1 us (4%)
  between operations  14.8 us (3%)
    psum x1, waiting for transfers between devices, per_device(): summed_w2, summed_b2 = lax.psum((local_w2, local_b2), ('sx', 'rep'))  75.9 us
    psum x1, blocking collectives, per_device(): summed_w1, summed_b1 = lax.psum((local_w1, local_b1), ('sx', 'sy', 'rep'))  66.4 us
    dot_general x54, matrix products, weight_terms(): jnp.einsum('oxyz,cxyz->oc', cotan, piece, preferred_element_type=jnp.floa...  48.6 us
    conv_general_dilated x11, local copies, waits for them, and re-layouts, convolve(): lax.conv_general_dilated(padded[None], kernel, (1, 1, 1), ((0, 0), (0, 0)...  45.9 us
    conv_general_dilated x3, matrix products, convolve(): lax.conv_general_dilated(padded[None], kernel, (1, 1, 1), ((0, 0), (0, 0)...  41.4 us
    psum x1, waiting for transfers between devices, per_device(): summed_w1, summed_b1 = lax.psum((local_w1, local_b1), ('sx', 'sy', 'rep'))  41.3 us
    all_gather x1, waiting for transfers between devices, per_device(): gathered = lax.all_gather(pooled_x, 'sy', axis=2, tiled=True)  40.3 us
    psum x1, blocking collectives, per_device(): summed_w2, summed_b2 = lax.psum((local_w2, local_b2), ('sx', 'rep'))  36.2 us
  transfers between devices with their start and end apart: 12, of which 9 were waited for; matrix products, arithmetic and copies ran while one was open for 33% of the time, Pallas kernels for 0%

commit v1 on v0

--- a/solution.py
+++ b/solution.py
@@ -69,7 +69,8 @@
     act = jnp.where(pre > 0, pre, 0.3 * pre)
     pooled = pool_mean(act).astype(jnp.bfloat16)
     pooled_x = padded_2(pooled, (("sx", 1),), 1)
-    gathered = lax.all_gather(pooled_x, "sy", axis=2, tiled=True)
+    sent = jnp.stack([pooled_x] * lax.axis_size("sy"))
+    gathered = jnp.concatenate(lax.all_to_all(sent, "sy", 0, 0), axis=2)
     pooled_pad = jnp.pad(gathered, ((0, 0), (0, 0), (1, 1), (1, 1)))
     second = convolve(pooled_pad, second_kernel, 0) + second_bias[:, None, None, None]
     second_out = second.astype(jnp.float32)

time: 545 us -> 500 us (0.917)
  waiting for transfers between devices: 177 us -> 134 us
  local copies, waits for them, and re-layouts: 97.9 us -> 109 us
  other arithmetic: 31.6 us -> 21.2 us
  starting transfers between devices: 21.1 us -> 27.1 us
    psum x1, waiting for transfers between devices: 75.9 us -> 32.2 us  [per_device(): summed_w2, summed_b2 = lax.psum((local_w2, local_b2), ('sx', 'rep'))]
    all_gather x1 -> x0, waiting for transfers between devices: 40.3 us -> none  [per_device(): gathered = lax.all_gather(pooled_x, 'sy', axis=2, tiled=True)]
    psum x1, waiting for transfers between devices: 41.3 us -> 77.1 us  [per_device(): summed_w1, summed_b1 = lax.psum((local_w1, local_b1), ('sx', 'sy', 'rep'))]
    concatenate x3, other arithmetic: 14.5 us -> 4.37 us  [padded_2(): jnp.concatenate([lax.ppermute(tail, axis, [(i, (i + 1) % count) for i in...]
    all_to_all x0 -> x1, starting transfers between devices: none -> 5.83 us  [per_device(): gathered = jnp.concatenate(lax.all_to_all(sent, 'sy', 0, 0), axis=2)]
    unnamed x51 -> x57, local copies, waits for them, and re-layouts: 25.9 us -> 27 us
  transfers between devices with their start and end apart: 12 -> 12, of which waited for: 9 -> 9; matrix products, arithmetic and copies ran while one was open for 33% -> 24% of each run, Pallas kernels for 0% -> 0%
where the time goes in v1:
time: 500 us; the launch traced here: 496 us
  waiting for transfers between devices  134 us (27%)
  local copies, waits for them, and re-layouts  109 us (22%)
  blocking collectives  99.2 us (20%)
  matrix products  88.9 us (18%)
  starting transfers between devices  27.1 us (5%)
  other arithmetic  21.2 us (4%)
  between operations  16.3 us (3%)
    psum x1, waiting for transfers between devices, per_device(): summed_w1, summed_b1 = lax.psum((local_w1, local_b1), ('sx', 'sy', 'rep'))  77.1 us
    psum x1, blocking collectives, per_device(): summed_w1, summed_b1 = lax.psum((local_w1, local_b1), ('sx', 'sy', 'rep'))  64.4 us
    conv_general_dilated x11, local copies, waits for them, and re-layouts, convolve(): lax.conv_general_dilated(padded[None], kernel, (1, 1, 1), ((0, 0), (0, 0)...  49.2 us
    dot_general x54, matrix products, weight_terms(): jnp.einsum('oxyz,cxyz->oc', cotan, piece, preferred_element_type=jnp.floa...  47 us
    conv_general_dilated x3, matrix products, convolve(): lax.conv_general_dilated(padded[None], kernel, (1, 1, 1), ((0, 0), (0, 0)...  41.9 us
    psum x1, blocking collectives, per_device(): summed_w2, summed_b2 = lax.psum((local_w2, local_b2), ('sx', 'rep'))  34.8 us
    psum x1, waiting for transfers between devices, per_device(): summed_w2, summed_b2 = lax.psum((local_w2, local_b2), ('sx', 'rep'))  32.2 us
    unnamed x57, local copies, waits for them, and re-layouts  27 us
  transfers between devices with their start and end apart: 12, of which 9 were waited for; matrix products, arithmetic and copies ran while one was open for 24% of the time, Pallas kernels for 0%

profile of v1, /device:TPU:1, one launch (start us, length us, event | category | flops | bytes accessed | tf_op | source)
XLA Modules:
  0.0 495.6 jit_solution(17816794567025119339)
XLA Ops:
  9.4 4.9 collective-permute-start
  17.7 4.4 collective-permute-done.1
  22.1 3.2 collective-permute-start.2
  26.6 3.7 collective-permute-done.3
  32.2 5.4 %reshape.256 = bf16[32,4,18,1,8,33]{5,4,0,2,1,3:T(8,128)(2,1)} reshape(bf16[32,4,18,1,264]{4,0,2,1,3:T(8,128)(2,1)S(1)} %pad.15) | data formatting | bytes 2433024 | tf_op jit(solution)/shard_map/conv_general_dilated | solution.py:26
  37.6 9.2 %copy.324 = bf16[32,4,18,1,8,33]{0,4,5,2,1,3:T(8,128)(2,1)} copy(bf16[32,4,18,1,8,33]{5,4,0,2,1,3:T(8,128)(2,1)} %reshape.256) | data formatting | bytes 2433024 | tf_op jit(solution)/shard_map/conv_general_dilated | solution.py:26
  47.9 12.3 %compare_select_fusion = (f32[2,16,8,33,64]{4,2,3,1,0:T(8,128)}, f32[2,16,8,33,64]{4,2,3,1,0:T(8,128)S(1)}, f32[2,16,8,33,64]{4,2,3,1,0:T(8,128)}) fusion(f32[64]{0:T(128)S(1)} %copy-done.20, bf16[64,32,3,3,3]{0,1,4,3,2:T(8,128)(2,1)S(1)} %copy-done, bf16[32,4,18,1,7,2]{0,4,5,2,1,3:T(8,128)(2,1)S(1)} %slice.262, bf16[32,4,18,1,8,33]{0,4,5,2,1,3:T(8,128)(2,1)} %copy.324, ...), kind=kOutput, calls=%fused_computation.44 | convolution fusion | flops 941395968 | bytes 7880200 | tf_op jit(solution)/shard_map/conv_general_dilated | solution.py:26
  63.4 3.2 collective-permute-start.4
  69.9 4.4 collective-permute-done.5
  75.0 2.5 stack.179
  77.5 5.8 %all-to-all-start = ((bf16[8,64,3,8,128]{4,1,3,2,0:T(8,128)(2,1)}), bf16[8,64,3,8,128]{4,1,3,2,0:T(8,128)(2,1)S(1)}, u32[]{:S(2)}, u32[]{:S(2)}) async-start(bf16[8,64,3,8,128]{4,1,3,2,0:T(8,128)(2,1)} %stack.179), calls=%async_computation | async-start | bytes 6291456 | tf_op jit(solution)/shard_map/all_to_all | solution.py:73
  89.1 3.9 collective-permute-done.6
  93.0 5.0 %collective-permute-done.7 = bf16[16,1,64,128]{2,0,3,1:T(8,128)(2,1)S(1)} collective-permute-done((bf16[16,1,64,128]{2,0,3,1:T(8,128)(2,1)}, bf16[16,1,64,128]{2,0,3,1:T(8,128)(2,1)S(1)}, u32[]{:S(2)}, u32[]{:S(2)}) %collective-permute-start.7) | collective-permute-done | bytes 262176 | tf_op jit(solution)/shard_map/ppermute | solution.py:18
  102.0 7.3 %copy.335 = bf16[16,3,66,1,8,17]{0,4,5,2,1,3:T(8,128)(2,1)} copy(bf16[16,3,66,1,8,17]{2,0,5,4,1,3:T(8,128)(2,1)} %bitcast.671) | data formatting | bytes 1723392 | tf_op jit(solution)/shard_map/conv_general_dilated | solution.py:26
  110.6 10.0 %broadcast_select_fusion = f32[1,64,8,17,64]{4,2,3,1,0:T(8,128)S(1)} fusion(pred[8,17]{0,1:T(8,128)(4,1)S(1)} %copy-done.23, bf16[16,64,3,3,3]{1,0,4,3,2:T(8,128)(2,1)} %param.9, bf16[16,3,66,1,7,2]{0,4,5,2,1,3:T(8,128)(2,1)S(1)} %slice.266, bf16[16,3,66,1,8,17]{0,4,5,2,1,3:T(8,128)(2,1)} %copy.335), kind=kOutput, calls=%fused_computation.70 | convolution fusion | flops 484742656 | bytes 3234056 | tf_op jit(solution)/shard_map/conv_general_dilated | solution.py:26
  120.7 2.8 copy.336
  125.2 2.8 copy.327
  142.1 4.8 slice_bitcast_fusion.1
  148.3 34.8 %psum.31 = f32[16]{0:T(128)S(1)} all-reduce(f32[16]{0:T(128)S(1)} %convert_reduce_fusion.1), channel_id=1, replica_groups=mesh['sx'=8,'sy'=8,'rep'=2] {'sx','rep'}, use_global_device_ids=true, to_apply=%region_8.9 | all-reduce | flops 16 | bytes 128 | tf_op jit(solution)/shard_map/psum | solution.py:84
  183.6 3.1 copy.338
  188.9 5.2 %copy.423 = f32[2,16,1,256,64]{3,1,0,4,2:T(8,128)} copy(f32[2,16,1,256,64]{4,1,3,0,2:T(8,128)} %slice.268) | data formatting | bytes 4194304
  194.1 5.2 %copy.353 = f32[2,16,8,33,64]{4,1,3,2,0:T(8,128)} copy(f32[2,16,8,33,64]{4,2,3,1,0:T(8,128)} %get-tuple-element.32) | data formatting | bytes 4325376 | tf_op jit(solution)/shard_map/jit(_where)/select_n | solution.py:86
  200.9 2.6 select_maximum_fusion
  203.5 5.2 %pad_bitcast_fusion = bf16[64,3,66,1,130]{4,0,2,1,3:T(8,128)(2,1)} fusion(bf16[64,3,64,128]{3,0,2,1:T(8,128)(2,1)S(1)} %bitcast.625), kind=kLoop, calls=%fused_computation.24 | loop fusion | bytes 6440448 | tf_op jit(solution)/shard_map/broadcast_in_dim | solution.py:27
  208.7 14.8 %copy.424 = bf16[64,3,66,1,130]{2,0,4,1,3:T(8,128)(2,1)} copy(bf16[64,3,66,1,130]{4,0,2,1,3:T(8,128)(2,1)} %pad_bitcast_fusion) | data formatting | bytes 6589440
  223.5 7.5 %pad.17.clone = bf16[64,3,66,1,136]{2,0,4,1,3:T(8,128)(2,1)} pad(bf16[64,3,66,1,130]{2,0,4,1,3:T(8,128)(2,1)} %copy.424, bf16[]{:T(256)} %constant.6.clone.1), padding=0_0x0_0x0_0x0_0x0_6 | pad | bytes 6741506 | tf_op jit(solution)/shard_map/broadcast_in_dim | solution.py:27
  231.0 11.7 %copy.330 = bf16[64,3,66,1,8,17]{0,4,5,2,1,3:T(8,128)(2,1)} copy(bf16[64,3,66,1,8,17]{2,0,5,4,1,3:T(8,128)(2,1)} %bitcast.653) | data formatting | bytes 6893568 | tf_op jit(solution)/shard_map/conv_general_dilated | solution.py:26
  244.1 19.5 %fusion.9 = f32[1,64,8,17,16]{4,2,3,1,0:T(8,128)} fusion(bf16[16,64,3,3,3]{1,0,4,3,2:T(8,128)(2,1)S(1)} %copy-done.21, bf16[64,3,66,1,7,2]{0,4,5,2,1,3:T(8,128)(2,1)S(1)} %slice.264, bf16[64,3,66,1,8,17]{0,4,5,2,1,3:T(8,128)(2,1)} %copy.330), kind=kOutput, calls=%fused_computation.36 | convolution fusion | flops 492853248 | bytes 4413952 | tf_op jit(solution)/shard_map/conv_general_dilated | solution.py:26
  263.7 3.5 copy.331
  268.8 32.2 %all-reduce.8.cloned.1.call-done = f32[16,64,3,3,3]{1,0,4,3,2:T(8,128)} async-done(((f32[16,64,3,3,3]{1,0,4,3,2:T(8,128)}), f32[16,64,3,3,3]{1,0,4,3,2:T(8,128)}) %all-reduce.8.cloned.1.call-update) | async-done | bytes 110608 | tf_op jit(solution)/shard_map/psum | solution.py:84
  344.1 64.4 %psum.29 = f32[64]{0:T(128)S(1)} all-reduce(f32[64]{0:T(128)S(1)} %get-tuple-element.30), channel_id=1, replica_groups=mesh['sx'=8,'sy'=8,'rep'=2] {'sx','sy','rep'}, use_global_device_ids=true, to_apply=%region_5.6 | all-reduce | flops 64 | bytes 512 | tf_op jit(solution)/shard_map/psum | solution.py:89
  409.0 77.1 %all-reduce.6.cloned.1.call-done = f32[64,32,3,3,3]{0,1,4,3,2:T(8,128)} async-done(((f32[64,32,3,3,3]{0,1,4,3,2:T(8,128)}), f32[64,32,3,3,3]{0,1,4,3,2:T(8,128)}) %all-reduce.6.cloned.1.call-update) | async-done | bytes 221200 | tf_op jit(solution)/shard_map/psum | solution.py:89
  (156 shorter events, 96.7 us)
Async XLA Ops:
  8.0 39.9 %copy-start = (bf16[64,32,3,3,3]{0,1,4,3,2:T(8,128)(2,1)S(1)}, bf16[64,32,3,3,3]{0,1,4,3,2:T(8,128)(2,1)}, u32[]{:S(2)}) copy-start(bf16[64,32,3,3,3]{0,1,4,3,2:T(8,128)(2,1)} %param.7) | copy-start | bytes 331780
  9.4 20.9 %copy-start.3 = (bf16[1,32,2,16,256]{4,1,3,2,0:T(8,128)(2,1)}, bf16[1,32,2,16,256]{4,1,3,2,0:T(8,128)(2,1)S(1)}, u32[]{:S(2)}) copy-start(bf16[1,32,2,16,256]{4,1,3,2,0:T(8,128)(2,1)S(1)} %copy.539) | copy-start | bytes 1572868
  9.4 8.2 %collective-permute-start = (bf16[32,1,16,256]{3,0,2,1:T(8,128)(2,1)S(1)}, bf16[32,1,16,256]{3,0,2,1:T(8,128)(2,1)S(1)}, u32[]{:S(2)}, u32[]{:S(2)}) collective-permute-start(bf16[32,1,16,256]{3,0,2,1:T(8,128)(2,1)S(1)} %get-tuple-element.38), channel_id=1, source_target_pairs={{0,16},{16,32},{32,48},{48,64},{64,80},{80,96},{96,112},{1,17},{17... | collective-permute-start | bytes 786440 | tf_op jit(solution)/shard_map/ppermute | solution.py:16
  14.4 7.7 %collective-permute-start.1 = (bf16[32,1,16,256]{3,0,2,1:T(8,128)(2,1)S(1)}, bf16[32,1,16,256]{3,0,2,1:T(8,128)(2,1)S(1)}, u32[]{:S(2)}, u32[]{:S(2)}) collective-permute-start(bf16[32,1,16,256]{3,0,2,1:T(8,128)(2,1)S(1)} %get-tuple-element.39), channel_id=1, source_target_pairs={{16,0},{32,16},{48,32},{64,48},{80,64},{96,80},{112,96},{17,1},{33... | collective-permute-start | bytes 786440 | tf_op jit(solution)/shard_map/ppermute | solution.py:18
  17.7 12.6 %copy-start.9 = (bf16[32,1,16,256]{3,0,2,1:T(8,128)(2,1)}, bf16[32,1,16,256]{3,0,2,1:T(8,128)(2,1)S(1)}, u32[]{:S(2)}) copy-start(bf16[32,1,16,256]{3,0,2,1:T(8,128)(2,1)S(1)} %collective-permute-done) | copy-start | bytes 786436
  22.1 8.3 %copy-start.7 = (bf16[32,1,16,256]{3,0,2,1:T(8,128)(2,1)}, bf16[32,1,16,256]{3,0,2,1:T(8,128)(2,1)S(1)}, u32[]{:S(2)}) copy-start(bf16[32,1,16,256]{3,0,2,1:T(8,128)(2,1)S(1)} %collective-permute-done.1) | copy-start | bytes 786436
  22.1 4.5 collective-permute-start.2
  25.3 5.0 %collective-permute-start.3 = (bf16[32,4,1,256]{3,0,2,1:T(8,128)(2,1)S(1)}, bf16[32,4,1,256]{3,0,2,1:T(8,128)(2,1)S(1)}, u32[]{:S(2)}, u32[]{:S(2)}) collective-permute-start(bf16[32,4,1,256]{3,0,2,1:T(8,128)(2,1)S(1)} %get-tuple-element.37), channel_id=1, source_target_pairs={{2,0},{4,2},{6,4},{8,6},{10,8},{12,10},{14,12},{3,1},{5,3},{7,5},{... | collective-permute-start | bytes 196616 | tf_op jit(solution)/shard_map/ppermute | solution.py:18
  37.6 10.3 %copy-start.20 = (f32[64]{0:T(128)S(1)}, f32[64]{0:T(128)}, u32[]{:S(2)}) copy-start(f32[64]{0:T(128)} %param.8) | copy-start | bytes 772
  37.6 10.3 %copy-start.22 = (pred[8,33]{0,1:T(8,128)(4,1)S(1)}, pred[8,33]{0,1:T(8,128)(4,1)}, u32[]{:S(2)}) copy-start(pred[8,33]{0,1:T(8,128)(4,1)} %constant.41) | copy-start | bytes 796
  63.4 6.5 %collective-permute-start.4 = (bf16[64,1,8,128]{0,2,3,1:T(8,128)(2,1)S(1)}, bf16[64,1,8,128]{0,2,3,1:T(8,128)(2,1)S(1)}, u32[]{:S(2)}, u32[]{:S(2)}) collective-permute-start(bf16[64,1,8,128]{0,2,3,1:T(8,128)(2,1)S(1)} %fusion.182), channel_id=1, source_target_pairs={{0,16},{16,32},{32,48},{48,64},{64,80},{80,96},{96,112},{1,17},{17... | collective-permute-start | bytes 393224 | tf_op jit(solution)/shard_map/ppermute | solution.py:16
  66.6 7.7 %collective-permute-start.5 = (bf16[64,1,8,128]{0,2,3,1:T(8,128)(2,1)S(1)}, bf16[64,1,8,128]{0,2,3,1:T(8,128)(2,1)S(1)}, u32[]{:S(2)}, u32[]{:S(2)}) collective-permute-start(bf16[64,1,8,128]{0,2,3,1:T(8,128)(2,1)S(1)} %fusion.182), channel_id=1, source_target_pairs={{16,0},{32,16},{48,32},{64,48},{80,64},{96,80},{112,96},{17,1},{33... | collective-permute-start | bytes 393224 | tf_op jit(solution)/shard_map/ppermute | solution.py:18
  77.5 5.9 %copy-start.2 = (bf16[1,16,1,64,128]{4,3,2,1,0:T(8,128)(2,1)S(1)}, bf16[1,16,1,64,128]{4,3,2,1,0:T(8,128)(2,1)}, u32[]{:S(2)}) copy-start(bf16[1,16,1,64,128]{4,3,2,1,0:T(8,128)(2,1)} %param.11) | copy-start | bytes 786436
  77.5 46.1 %all-to-all-start = ((bf16[8,64,3,8,128]{4,1,3,2,0:T(8,128)(2,1)}), bf16[8,64,3,8,128]{4,1,3,2,0:T(8,128)(2,1)S(1)}, u32[]{:S(2)}, u32[]{:S(2)}) async-start(bf16[8,64,3,8,128]{4,1,3,2,0:T(8,128)(2,1)} %stack.179), calls=%async_computation | async-start | bytes 6291456 | tf_op jit(solution)/shard_map/all_to_all | solution.py:73
  83.3 217.7 %all-reduce.8.cloned.1.call-start = ((), (), s32[]{:S(2)}) async-start(), calls=%async_computation.4 | async-start | bytes 442368 | tf_op jit(solution)/shard_map/psum | solution.py:84
  84.5 8.4 %collective-permute-start.6 = (bf16[16,1,64,128]{2,0,3,1:T(8,128)(2,1)}, bf16[16,1,64,128]{2,0,3,1:T(8,128)(2,1)S(1)}, u32[]{:S(2)}, u32[]{:S(2)}) collective-permute-start(bf16[16,1,64,128]{2,0,3,1:T(8,128)(2,1)} %bitcast.672), channel_id=1, source_target_pairs={{0,16},{16,32},{32,48},{48,64},{64,80},{80,96},{96,112},{1,17},{17... | collective-permute-start | bytes 786440 | tf_op jit(solution)/shard_map/ppermute | solution.py:16
  86.8 11.2 %collective-permute-start.7 = (bf16[16,1,64,128]{2,0,3,1:T(8,128)(2,1)}, bf16[16,1,64,128]{2,0,3,1:T(8,128)(2,1)S(1)}, u32[]{:S(2)}, u32[]{:S(2)}) collective-permute-start(bf16[16,1,64,128]{2,0,3,1:T(8,128)(2,1)} %bitcast.673), channel_id=1, source_target_pairs={{16,0},{32,16},{48,32},{64,48},{80,64},{96,80},{112,96},{17,1},{33... | collective-permute-start | bytes 786440 | tf_op jit(solution)/shard_map/ppermute | solution.py:18
  102.0 8.6 %copy-start.23 = (pred[8,17]{0,1:T(8,128)(4,1)S(1)}, pred[8,17]{0,1:T(8,128)(4,1)}, u32[]{:S(2)}) copy-start(pred[8,17]{0,1:T(8,128)(4,1)} %constant.43) | copy-start | bytes 412
  141.9 160.8 %reduce-scatter.2.cloned.1.call-start = ((), (), s32[]{:S(2)}) async-start(), calls=%async_computation.2 | async-start | bytes 4718592 | tf_op jit(solution)/shard_map/reduce_scatter | solution.py:83
  146.9 339.2 %all-reduce.6.cloned.1.call-start = ((), (), s32[]{:S(2)}) async-start(), calls=%async_computation.3 | async-start | bytes 884736 | tf_op jit(solution)/shard_map/psum | solution.py:89
  194.1 5.2 %copy-start.4 = (bf16[1,32,2,16,256]{4,1,3,2,0:T(8,128)(2,1)S(1)}, bf16[1,32,2,16,256]{4,1,3,2,0:T(8,128)(2,1)}, u32[]{:S(2)}) copy-start(bf16[1,32,2,16,256]{4,1,3,2,0:T(8,128)(2,1)} %copy-done.3) | copy-start | bytes 1572868
  194.1 5.2 %copy-start.8 = (bf16[32,1,16,256]{3,0,2,1:T(8,128)(2,1)S(1)}, bf16[32,1,16,256]{3,0,2,1:T(8,128)(2,1)}, u32[]{:S(2)}) copy-start(bf16[32,1,16,256]{3,0,2,1:T(8,128)(2,1)} %copy-done.7) | copy-start | bytes 786436
  194.1 5.2 %copy-start.10 = (bf16[32,1,16,256]{3,0,2,1:T(8,128)(2,1)S(1)}, bf16[32,1,16,256]{3,0,2,1:T(8,128)(2,1)}, u32[]{:S(2)}) copy-start(bf16[32,1,16,256]{3,0,2,1:T(8,128)(2,1)} %copy-done.9) | copy-start | bytes 786436
  231.0 13.1 %copy-start.21 = (bf16[16,64,3,3,3]{1,0,4,3,2:T(8,128)(2,1)S(1)}, bf16[16,64,3,3,3]{1,0,4,3,2:T(8,128)(2,1)}, u32[]{:S(2)}) copy-start(bf16[16,64,3,3,3]{1,0,4,3,2:T(8,128)(2,1)} %param.9) | copy-start | bytes 165892
  263.7 3.6 copy-start.18
  263.7 3.6 copy-start.19
  309.1 3.8 copy-start.5
  309.1 3.8 copy-start.11
  312.9 3.8 copy-start.13
  315.5 9.0 %slice-start = ((s8[4325376]{0:T(1024)(128)(4,1)}), s8[4194304]{0:T(1024)(128)(4,1)S(1)}, s32[]{:S(2)}) async-start(s8[4325376]{0:T(1024)(128)(4,1)} %bitcast.665), calls=%async_computation.5 | async-start | bytes 8388608
  319.5 5.1 %slice-start.1 = ((s8[4325376]{0:T(1024)(128)(4,1)}), s8[131072]{0:T(1024)(128)(4,1)S(1)}, s32[]{:S(2)}) async-start(s8[4325376]{0:T(1024)(128)(4,1)} %bitcast.665), calls=%async_computation.6 | async-start | bytes 262144
  339.5 148.5 %copy-start.1 = (bf16[64,32,3,3,3]{0,1,4,3,2:T(8,128)(2,1)S(1)}, bf16[64,32,3,3,3]{0,1,4,3,2:T(8,128)(2,1)}, u32[]{:S(2)}) copy-start(bf16[64,32,3,3,3]{0,1,4,3,2:T(8,128)(2,1)} %param.7) | copy-start | bytes 331780
  (6 other events, 9.9 us)
Sparse Core Ops, SparseCore 0:
  142.0 158.9 all-reduce.7
Sparse Core Ops, SparseCore 1:
  147.0 57.2 reduce-scatter.1
  344.2 141.9 all-reduce.5
